TPU v7x, 256 devices: a whole 4x4x8 slice. The times are simulated.
256 devices in a mesh: dp: 8 (over z), section: 4 (over y_hi, core), seq: 8 (over y_lo, x).
Axes of the slice: x: 4, y: 4 (y_hi: 2, y_lo: 2; y = y_hi * 2 + y_lo), z: 8, core: 2. Of those that a mesh axis runs over, the one named last changes fastest.
Arguments:
- acts: bfloat16 [8, 1024, 1536], P('dp', 'seq'), may hold values from -6 to 6
- cotangent: bfloat16 [8, 1024, 1536], P('dp', 'seq'), may hold values from -6 to 6
- gains: bfloat16 [4, 1536], P('section'), may hold values from 0.5 to 1.5
- w_query: bfloat16 [4, 1536, 256], P('section'), may hold values from -0.15625 to 0.15625
- w_key: bfloat16 [4, 1536, 256], P('section'), may hold values from -0.15625 to 0.15625
- w_value: bfloat16 [4, 1536, 384], P('section'), may hold values from -0.15625 to 0.15625
- w_out: bfloat16 [4, 1536, 384], P('section'), may hold values from -0.3125 to 0.3125
Outputs:
- d_acts: bfloat16 [8, 1024, 1536], P('dp', 'seq', 'section')
- g_gains: float32 [4, 1536], P('section', ('dp', 'seq'))
- g_query: float32 [4, 1536, 256], P('section', ('dp', 'seq'))
- g_key: float32 [4, 1536, 256], P('section', ('dp', 'seq'))
- g_value: float32 [4, 1536, 384], P('section', ('dp', 'seq'))
- g_out: float32 [4, 1536, 384], P('section', ('dp', 'seq'))
All inputs are finite; a program needn't handle non-finite values.
Results may differ from a plain program's by a relative error of at most 0.02.
Values may be sent and summed in bfloat16 or wider, within the bound.
No kernel may reach another device: no remote copies, remote signals or barrier semaphores. Data moves between devices by JAX's collectives and lax.ppermute only.
A program may use at most 64 MiB of HBM per device.

v0:
```python
import jax
import jax.numpy as jnp
from jax import lax
from jax.sharding import PartitionSpec as P

HEADS = 4
KEY = 64
VALUE = 96
epsilon = 1e-05


def passed_along(block, axis, distance):
    devices = range(lax.axis_size(axis))
    route = [(i - distance, i) for i in devices if i - distance in devices]
    return lax.ppermute(block, axis, route)


def from_root(block, axis, owner):
    block = jnp.where(lax.axis_index(axis) == owner, block, jnp.zeros_like(block))
    return lax.psum(block, axis)


def layer_norm(inputs, norm_gain):
    widened = inputs.astype(jnp.float32)
    centred = widened - jnp.mean(widened, axis=-1, keepdims=True)
    inverse = lax.rsqrt(jnp.mean(centred * centred, axis=-1, keepdims=True) + epsilon)
    normed = centred * inverse
    return ((normed * norm_gain.astype(jnp.float32)).astype(jnp.bfloat16), normed, inverse)


def split_heads(matrix, width):
    return matrix.reshape(matrix.shape[0], HEADS, width)


def times_transposed(left, right):
    return jnp.einsum("ic,dc->id", left, right, preferred_element_type=jnp.float32)


def outer_sum(left, right):
    return jnp.einsum("id,ic->dc", left, right, preferred_element_type=jnp.float32)


def exp_scores_of(query_local, key_all):
    score_scale = KEY ** (-0.5)
    raw_scores = jnp.einsum(
        "ihc,jhc->hij",
        split_heads(query_local, KEY),
        split_heads(key_all, KEY),
        preferred_element_type=jnp.float32,
    )
    return jnp.exp(raw_scores * score_scale)


def forward_layer(inputs, weights):
    norm_gain, proj_query, proj_key, proj_value, proj_out = weights
    row_count = inputs.shape[0]
    normal_bf, normed, inverse = layer_norm(inputs, norm_gain)
    query_local = jnp.dot(normal_bf, proj_query, preferred_element_type=jnp.float32).astype(
        jnp.bfloat16
    )
    key_local = jnp.dot(normal_bf, proj_key, preferred_element_type=jnp.float32).astype(
        jnp.bfloat16
    )
    value_local = jnp.dot(normal_bf, proj_value, preferred_element_type=jnp.float32).astype(
        jnp.bfloat16
    )
    key_all, value_all = (
        lax.all_gather(key_local, "seq", axis=0, tiled=True),
        lax.all_gather(value_local, "seq", axis=0, tiled=True),
    )
    expo = exp_scores_of(query_local, key_all)
    totals = jnp.sum(expo, axis=-1)
    rounded = expo.astype(jnp.bfloat16)
    numerator = jnp.einsum(
        "hij,jhc->ihc", rounded, split_heads(value_all, VALUE), preferred_element_type=jnp.float32
    )
    attended = (
        (numerator / totals.T[:, :, None]).astype(jnp.bfloat16).reshape(row_count, HEADS * VALUE)
    )
    mixed_out = inputs.astype(jnp.float32) + times_transposed(attended, proj_out)
    record = (
        normal_bf,
        normed,
        inverse,
        query_local,
        key_local,
        value_local,
        key_all,
        value_all,
        totals,
        attended,
    )
    return (mixed_out.astype(jnp.bfloat16), record)


def backward_layer(grad_in, record, weights):
    norm_gain, proj_query, proj_key, proj_value, proj_out = weights
    (
        normal_bf,
        normed,
        inverse,
        query_local,
        key_local,
        value_local,
        key_all,
        value_all,
        totals,
        attended,
    ) = record
    row_count = grad_in.shape[0]
    score_scale = KEY ** (-0.5)
    grad_out_w = outer_sum(grad_in, attended)
    grad_attended = jnp.dot(grad_in, proj_out, preferred_element_type=jnp.float32).astype(
        jnp.bfloat16
    )
    grad_scaled = (
        split_heads(grad_attended, VALUE).astype(jnp.float32) / totals.T[:, :, None]
    ).astype(jnp.bfloat16)
    correction = jnp.sum(
        grad_scaled.astype(jnp.float32) * split_heads(attended, VALUE).astype(jnp.float32), axis=-1
    ).astype(jnp.bfloat16)
    query_heads = split_heads(query_local, KEY)
    expo = exp_scores_of(query_local, key_all)
    grad_probs = jnp.einsum(
        "ihc,jhc->hij",
        grad_scaled,
        split_heads(value_all, VALUE),
        preferred_element_type=jnp.float32,
    )
    grad_scores = (
        expo * (grad_probs - correction.astype(jnp.float32).T[:, :, None]) * score_scale
    ).astype(jnp.bfloat16)
    grad_query = jnp.einsum(
        "hij,jhc->ihc", grad_scores, split_heads(key_all, KEY), preferred_element_type=jnp.float32
    )
    grad_query = grad_query.astype(jnp.bfloat16).reshape(row_count, HEADS * KEY)
    rounded = expo.astype(jnp.bfloat16)
    part_key = jnp.einsum(
        "hij,ihc->jhc", grad_scores, query_heads, preferred_element_type=jnp.float32
    )
    part_value = jnp.einsum(
        "hij,ihc->jhc", rounded, grad_scaled, preferred_element_type=jnp.float32
    )
    full_rows = part_key.shape[0]
    key_sum, value_sum = (
        lax.psum_scatter(
            part_key.reshape(full_rows, HEADS * KEY).astype(jnp.bfloat16),
            "seq",
            scatter_dimension=0,
            tiled=True,
        ).astype(jnp.float32),
        lax.psum_scatter(
            part_value.reshape(full_rows, HEADS * VALUE).astype(jnp.bfloat16),
            "seq",
            scatter_dimension=0,
            tiled=True,
        ).astype(jnp.float32),
    )
    grad_key = key_sum.astype(jnp.bfloat16)
    grad_value = value_sum.astype(jnp.bfloat16)
    grad_query_w = outer_sum(normal_bf, grad_query)
    grad_key_w = outer_sum(normal_bf, grad_key)
    grad_value_w = outer_sum(normal_bf, grad_value)
    grad_normal = times_transposed(grad_query, proj_query)
    grad_normal = grad_normal + times_transposed(grad_key, proj_key)
    grad_normal = grad_normal + times_transposed(grad_value, proj_value)
    grad_gain = jnp.sum(grad_normal * normed, axis=0)
    grad_normed = grad_normal * norm_gain.astype(jnp.float32)
    grad_inputs = inverse * (
        grad_normed
        - jnp.mean(grad_normed, axis=-1, keepdims=True)
        - normed * jnp.mean(grad_normed * normed, axis=-1, keepdims=True)
    )
    passed = (grad_in.astype(jnp.float32) + grad_inputs).astype(jnp.bfloat16)
    return (passed, (grad_gain, grad_query_w, grad_key_w, grad_value_w, grad_out_w))


def shards(acts, cotangent, gains, w_query, w_key, w_value, w_out):
    weights = (gains[0], w_query[0], w_key[0], w_value[0], w_out[0])
    section_now = lax.axis_index("section")
    section_count = lax.axis_size("section")
    inputs = acts[0]
    saved = None
    for section_step in range(section_count):
        output, record = forward_layer(inputs, weights)
        if section_step == 0:
            saved = record
        else:
            saved = jax.tree.map(
                lambda latest, earlier: jnp.where(section_now == section_step, latest, earlier),
                record,
                saved,
            )
        if section_step + 1 < section_count:
            inputs = passed_along(output, "section", 1)
    grad_flow = cotangent[0]
    grad_terms = None
    passed = grad_flow
    for section_step in reversed(range(section_count)):
        passed, fresh_terms = backward_layer(grad_flow, saved, weights)
        if section_step == section_count - 1:
            grad_terms = fresh_terms
        else:
            grad_terms = jax.tree.map(
                lambda latest, earlier: jnp.where(section_now == section_step, latest, earlier),
                fresh_terms,
                grad_terms,
            )
        if section_step > 0:
            grad_flow = passed_along(passed, "section", -1)
    input_grad = from_root(passed, "section", 0)
    channel_share = input_grad.shape[1] // section_count
    own_channels = lax.dynamic_slice_in_dim(
        input_grad, section_now * channel_share, channel_share, 1
    )
    grad_gain, grad_query_w, grad_key_w, grad_value_w, grad_out_w = grad_terms
    sums = (
        lax.psum_scatter(grad_gain[None], ("dp", "seq"), scatter_dimension=1, tiled=True),
        lax.psum_scatter(grad_query_w[None], ("dp", "seq"), scatter_dimension=1, tiled=True),
        lax.psum_scatter(grad_key_w[None], ("dp", "seq"), scatter_dimension=1, tiled=True),
        lax.psum_scatter(grad_value_w[None], ("dp", "seq"), scatter_dimension=1, tiled=True),
        lax.psum_scatter(grad_out_w[None], ("dp", "seq"), scatter_dimension=1, tiled=True),
    )
    return (own_channels[None], sums[0], sums[1], sums[2], sums[3], sums[4])


def solution(mesh):
    return jax.shard_map(
        shards,
        mesh=mesh,
        in_specs=(
            P("dp", "seq", None),
            P("dp", "seq", None),
            P("section", None),
            P("section", None, None),
            P("section", None, None),
            P("section", None, None),
            P("section", None, None),
        ),
        out_specs=(
            P("dp", "seq", "section"),
            P("section", ("dp", "seq")),
            P("section", ("dp", "seq"), None),
            P("section", ("dp", "seq"), None),
            P("section", ("dp", "seq"), None),
            P("section", ("dp", "seq"), None),
        ),
        check_vma=False,
    )
```

profile of v0, /device:TPU:16, one launch (start us, length us, event | category | flops | bytes accessed | tf_op | source)
XLA Modules:
  0.0 2088.0 jit_solution(8954973873401913931)
XLA Ops:
  13.6 29.1 %all_gather.25 = bf16[1024,256]{1,0:T(8,128)(2,1)S(1)} all-gather(bf16[128,256]{1,0:T(8,128)(2,1)S(1)} %convolution_convert_fusion.14), channel_id=1, replica_groups=mesh['dp'=8,'section'=4,'seq'=8] {'seq'}, dimensions={0}, use_global_device_ids=true | all-gather | bytes 589824 | tf_op jit(solution)/shard_map/all_gather | solution.py:68
  43.6 29.5 %all_gather.24 = bf16[1024,384]{1,0:T(8,128)(2,1)S(1)} all-gather(bf16[128,384]{1,0:T(8,128)(2,1)S(1)} %fusion.52), channel_id=1, replica_groups=mesh['dp'=8,'section'=4,'seq'=8] {'seq'}, dimensions={0}, use_global_device_ids=true | all-gather | bytes 884736 | tf_op jit(solution)/shard_map/all_gather | solution.py:69
  79.7 8.7 collective-permute-done
  93.6 31.0 %all_gather.27 = bf16[1024,256]{1,0:T(8,128)(2,1)} all-gather(bf16[128,256]{1,0:T(8,128)(2,1)S(1)} %convolution_convert_fusion.12), channel_id=1, replica_groups=mesh['dp'=8,'section'=4,'seq'=8] {'seq'}, dimensions={0}, use_global_device_ids=true | all-gather | bytes 589824 | tf_op jit(solution)/shard_map/all_gather | solution.py:68
  127.7 31.3 %all_gather.26 = bf16[1024,384]{1,0:T(8,128)(2,1)} all-gather(bf16[128,384]{1,0:T(8,128)(2,1)S(1)} %fusion.55), channel_id=1, replica_groups=mesh['dp'=8,'section'=4,'seq'=8] {'seq'}, dimensions={0}, use_global_device_ids=true | all-gather | bytes 884736 | tf_op jit(solution)/shard_map/all_gather | solution.py:69
  159.0 2.3 copy.67
  166.0 9.0 collective-permute-done.1
  180.3 30.8 %all_gather.29 = bf16[1024,256]{1,0:T(8,128)(2,1)} all-gather(bf16[128,256]{1,0:T(8,128)(2,1)S(1)} %convolution_convert_fusion.10), channel_id=1, replica_groups=mesh['dp'=8,'section'=4,'seq'=8] {'seq'}, dimensions={0}, use_global_device_ids=true | all-gather | bytes 589824 | tf_op jit(solution)/shard_map/all_gather | solution.py:68
  214.4 31.3 %all_gather.28 = bf16[1024,384]{1,0:T(8,128)(2,1)} all-gather(bf16[128,384]{1,0:T(8,128)(2,1)S(1)} %fusion.58), channel_id=1, replica_groups=mesh['dp'=8,'section'=4,'seq'=8] {'seq'}, dimensions={0}, use_global_device_ids=true | all-gather | bytes 884736 | tf_op jit(solution)/shard_map/all_gather | solution.py:69
  245.6 2.3 copy.70
  257.2 5.4 collective-permute-done.2
  265.7 28.9 %all_gather.30 = bf16[1024,256]{1,0:T(8,128)(2,1)S(1)} all-gather(bf16[128,256]{1,0:T(8,128)(2,1)S(1)} %convolution_convert_fusion.9), channel_id=1, replica_groups=mesh['dp'=8,'section'=4,'seq'=8] {'seq'}, dimensions={0}, use_global_device_ids=true | all-gather | bytes 589824 | tf_op jit(solution)/shard_map/all_gather | solution.py:68
  299.6 29.4 %all_gather.31 = bf16[1024,384]{1,0:T(8,128)(2,1)S(1)} all-gather(bf16[128,384]{1,0:T(8,128)(2,1)S(1)} %fusion.61), channel_id=1, replica_groups=mesh['dp'=8,'section'=4,'seq'=8] {'seq'}, dimensions={0}, use_global_device_ids=true | all-gather | bytes 884736 | tf_op jit(solution)/shard_map/all_gather | solution.py:69
  331.0 2.3 copy.79
  339.3 2.4 copy.78
  352.1 2.3 copy.87
  358.2 36.1 %reduce-scatter.42.cloned.1.call-done = bf16[128,256]{1,0:T(8,128)(2,1)} async-done(((bf16[1024,256]{1,0:T(8,128)(2,1)}), bf16[128,256]{1,0:T(8,128)(2,1)}) %reduce-scatter.42.cloned.1.call-update) | async-done | bytes 65552
  394.3 2.4 convolution_add_fusion.7
  396.8 40.3 %reduce-scatter.44.cloned.1.call-done = bf16[128,384]{1,0:T(8,128)(2,1)} async-done(((bf16[1024,384]{1,0:T(8,128)(2,1)}), bf16[128,384]{1,0:T(8,128)(2,1)}) %reduce-scatter.44.cloned.1.call-update) | async-done | bytes 98320
  437.1 3.1 multiply_reduce_fusion
  442.4 5.3 collective-permute-done.3
  452.3 2.4 multiply_convert_fusion.2
  458.8 2.5 convolution_convert_fusion.2
  461.4 2.3 copy.91
  467.6 31.4 %reduce-scatter.46.cloned.1.call-done = bf16[128,256]{1,0:T(8,128)(2,1)} async-done(((bf16[1024,256]{1,0:T(8,128)(2,1)}), bf16[128,256]{1,0:T(8,128)(2,1)}) %reduce-scatter.46.cloned.1.call-update) | async-done | bytes 65552
  499.0 2.7 convolution_add_fusion.5
  501.7 39.9 %reduce-scatter.48.cloned.1.call-done = bf16[128,384]{1,0:T(8,128)(2,1)} async-done(((bf16[1024,384]{1,0:T(8,128)(2,1)}), bf16[128,384]{1,0:T(8,128)(2,1)}) %reduce-scatter.48.cloned.1.call-update) | async-done | bytes 98320
  541.6 2.4 multiply_reduce_fusion.1
  546.2 5.3 collective-permute-done.4
  556.1 2.4 multiply_convert_fusion.1
  562.9 2.5 convolution_convert_fusion.1
  571.6 31.2 %reduce-scatter.50.cloned.1.call-done = bf16[128,256]{1,0:T(8,128)(2,1)} async-done(((bf16[1024,256]{1,0:T(8,128)(2,1)}), bf16[128,256]{1,0:T(8,128)(2,1)}) %reduce-scatter.50.cloned.1.call-update) | async-done | bytes 65552
  602.8 2.6 convolution_add_fusion.3
  605.4 40.0 %reduce-scatter.52.cloned.1.call-done = bf16[128,384]{1,0:T(8,128)(2,1)} async-done(((bf16[1024,384]{1,0:T(8,128)(2,1)}), bf16[128,384]{1,0:T(8,128)(2,1)}) %reduce-scatter.52.cloned.1.call-update) | async-done | bytes 98320
  645.4 2.4 multiply_reduce_fusion.2
  650.1 5.3 collective-permute-done.5
  659.8 2.3 multiply_convert_fusion
  668.5 2.4 copy.99
  673.1 2.5 fusion.174
  679.0 27.4 %reduce-scatter.54.cloned.1.call-done = bf16[128,256]{1,0:T(8,128)(2,1)} async-done(((bf16[1024,256]{1,0:T(8,128)(2,1)}), bf16[128,256]{1,0:T(8,128)(2,1)}) %reduce-scatter.54.cloned.1.call-update) | async-done | bytes 65552
  706.4 2.5 convolution_add_fusion.1
  708.8 40.3 %reduce-scatter.56.cloned.1.call-done = bf16[128,384]{1,0:T(8,128)(2,1)} async-done(((bf16[1024,384]{1,0:T(8,128)(2,1)}), bf16[128,384]{1,0:T(8,128)(2,1)}) %reduce-scatter.56.cloned.1.call-update) | async-done | bytes 98320
  753.4 3.0 fusion.8
  771.8 157.9 %all-reduce = f32[1,1536]{1,0:T(1,128)S(1)} all-reduce(f32[1,1536]{1,0:T(1,128)S(1)} %select_n.362), channel_id=10, replica_groups=mesh['dp'=8,'section'=4,'seq'=8] {'dp','seq'}, use_global_device_ids=true, to_apply=%region_37.38.clone | all-reduce | flops 1536 | bytes 12288
  931.9 188.5 %reduce-scatter.38.cloned.1.call-done = f32[1,24,256]{2,1,0:T(8,128)} async-done(((f32[1,1536,256]{2,1,0:T(8,128)}), f32[1,24,256]{2,1,0:T(8,128)}) %reduce-scatter.38.cloned.1.call-update) | async-done | bytes 24592 | tf_op jit(solution)/shard_map/reduce_scatter | solution.py:219
  1120.3 318.8 %reduce-scatter.40.cloned.1.call-done = f32[1,24,256]{2,1,0:T(8,128)} async-done(((f32[1,1536,256]{2,1,0:T(8,128)}), f32[1,24,256]{2,1,0:T(8,128)}) %reduce-scatter.40.cloned.1.call-update) | async-done | bytes 24592 | tf_op jit(solution)/shard_map/reduce_scatter | solution.py:220
  1439.1 320.8 %reduce-scatter.60.cloned.1.call-done = f32[1,24,384]{2,1,0:T(8,128)} async-done(((f32[1,1536,384]{2,1,0:T(8,128)}), f32[1,24,384]{2,1,0:T(8,128)}) %reduce-scatter.60.cloned.1.call-update) | async-done | bytes 36880
  1759.9 321.2 %reduce-scatter.58.cloned.1.call-done = f32[1,24,384]{2,1,0:T(8,128)} async-done(((f32[1,1536,384]{2,1,0:T(8,128)}), f32[1,24,384]{2,1,0:T(8,128)}) %reduce-scatter.58.cloned.1.call-update) | async-done | bytes 36880
  (382 shorter events, 145.7 us)
Async XLA Ops:
  7.2 5.9 copy-start
  7.2 5.6 copy-start.27
  7.2 5.6 copy-start.14
  7.2 387.1 %reduce-scatter.42.cloned.1.call-start = ((), (), s32[]{:S(2)}) async-start(), calls=%async_computation.15 | async-start | bytes 589824
  8.5 5.0 copy-start.101
  42.6 33.4 %copy-start.33 = (bf16[1024,256]{1,0:T(8,128)(2,1)}, bf16[1024,256]{1,0:T(8,128)(2,1)S(1)}, u32[]{:S(2)}) copy-start(bf16[1024,256]{1,0:T(8,128)(2,1)S(1)} %all_gather.25) | copy-start | bytes 1572868
  76.5 11.9 copy-start.58
  76.5 13.0 copy-start.9
  77.8 10.6 collective-permute-start
  88.4 75.1 %copy-start.29 = (bf16[128,1536]{1,0:T(8,128)(2,1)}, bf16[128,1536]{1,0:T(8,128)(2,1)S(1)}, u32[]{:S(2)}) copy-start(bf16[128,1536]{1,0:T(8,128)(2,1)S(1)} %collective-permute-done) | copy-start | bytes 1179652
  88.8 37.8 %copy-start.99 = (f32[128]{0:T(128)}, f32[128]{0:T(128)S(1)}, u32[]{:S(2)}) copy-start(f32[128]{0:T(128)S(1)} %fusion.117) | copy-start | bytes 1540
  163.5 11.5 copy-start.61
  164.1 11.0 collective-permute-start.1
  175.0 75.2 %copy-start.31 = (bf16[128,1536]{1,0:T(8,128)(2,1)}, bf16[128,1536]{1,0:T(8,128)(2,1)S(1)}, u32[]{:S(2)}) copy-start(bf16[128,1536]{1,0:T(8,128)(2,1)S(1)} %collective-permute-done.1) | copy-start | bytes 1179652
  175.4 37.8 %copy-start.100 = (f32[128]{0:T(128)}, f32[128]{0:T(128)S(1)}, u32[]{:S(2)}) copy-start(f32[128]{0:T(128)S(1)} %fusion.116) | copy-start | bytes 1540
  251.5 11.2 collective-permute-start.2
  257.2 38.2 %copy-start.34 = (bf16[1024,256]{1,0:T(8,128)(2,1)S(1)}, bf16[1024,256]{1,0:T(8,128)(2,1)}, u32[]{:S(2)}) copy-start(bf16[1024,256]{1,0:T(8,128)(2,1)} %copy-done.33) | copy-start | bytes 1572868
  257.2 38.2 %copy-start.35 = (bf16[1024,256]{1,0:T(8,128)(2,1)S(1)}, bf16[1024,256]{1,0:T(8,128)(2,1)}, u32[]{:S(2)}) copy-start(bf16[1024,256]{1,0:T(8,128)(2,1)} %all_gather.27) | copy-start | bytes 1572868
  257.2 38.2 %copy-start.36 = (bf16[1024,256]{1,0:T(8,128)(2,1)S(1)}, bf16[1024,256]{1,0:T(8,128)(2,1)}, u32[]{:S(2)}) copy-start(bf16[1024,256]{1,0:T(8,128)(2,1)} %all_gather.29) | copy-start | bytes 1572868
  262.6 70.7 %copy-start.40 = (bf16[128,1536]{1,0:T(8,128)(2,1)}, bf16[128,1536]{1,0:T(8,128)(2,1)S(1)}, u32[]{:S(2)}) copy-start(bf16[128,1536]{1,0:T(8,128)(2,1)S(1)} %collective-permute-done.2) | copy-start | bytes 1179652
  265.7 32.6 %copy-start.107 = (f32[128]{0:T(128)S(1)}, f32[128]{0:T(128)}, u32[]{:S(2)}) copy-start(f32[128]{0:T(128)} %copy-done.106) | copy-start | bytes 1540
  298.4 31.6 %copy-start.23 = (bf16[1024,384]{1,0:T(8,128)(2,1)S(1)}, bf16[1024,384]{1,0:T(8,128)(2,1)}, u32[]{:S(2)}) copy-start(bf16[1024,384]{1,0:T(8,128)(2,1)} %copy-done.22) | copy-start | bytes 2359300
  298.4 31.6 %copy-start.24 = (bf16[1024,384]{1,0:T(8,128)(2,1)S(1)}, bf16[1024,384]{1,0:T(8,128)(2,1)}, u32[]{:S(2)}) copy-start(bf16[1024,384]{1,0:T(8,128)(2,1)} %all_gather.26) | copy-start | bytes 2359300
  298.4 31.6 %copy-start.25 = (bf16[1024,384]{1,0:T(8,128)(2,1)S(1)}, bf16[1024,384]{1,0:T(8,128)(2,1)}, u32[]{:S(2)}) copy-start(bf16[1024,384]{1,0:T(8,128)(2,1)} %all_gather.28) | copy-start | bytes 2359300
  335.2 6.5 copy-start.56
  336.2 9.6 copy-start.52
  344.6 5.4 copy-start.3
  349.9 87.1 %reduce-scatter.44.cloned.1.call-start = ((), (), s32[]{:S(2)}) async-start(), calls=%async_computation.16 | async-start | bytes 884736
  354.5 144.5 %reduce-scatter.46.cloned.1.call-start = ((), (), s32[]{:S(2)}) async-start(), calls=%async_computation.17 | async-start | bytes 589824
  356.3 38.0 %copy-start.15 = (bf16[1,1536,256]{2,1,0:T(8,128)(2,1)S(1)}, bf16[1,1536,256]{2,1,0:T(8,128)(2,1)}, u32[]{:S(2)}) copy-start(bf16[1,1536,256]{2,1,0:T(8,128)(2,1)} %param.11) | copy-start | bytes 2359300
  356.4 80.7 %copy-start.28 = (bf16[1,128,1536]{2,1,0:T(8,128)(2,1)S(1)}, bf16[1,128,1536]{2,1,0:T(8,128)(2,1)}, u32[]{:S(2)}) copy-start(bf16[1,128,1536]{2,1,0:T(8,128)(2,1)} %param.7) | copy-start | bytes 1179652
  396.8 43.4 %copy-start.95 = (f32[128]{0:T(128)S(1)}, f32[128]{0:T(128)}, u32[]{:S(2)}) copy-start(f32[128]{0:T(128)} %get-tuple-element.28) | copy-start | bytes 1540
  440.4 7.2 collective-permute-start.3
  458.8 82.8 %reduce-scatter.48.cloned.1.call-start = ((), (), s32[]{:S(2)}) async-start(), calls=%async_computation.18 | async-start | bytes 884736
  463.7 139.1 %reduce-scatter.50.cloned.1.call-start = ((), (), s32[]{:S(2)}) async-start(), calls=%async_computation.19 | async-start | bytes 589824
  544.3 7.2 collective-permute-start.4
  562.6 82.8 %reduce-scatter.52.cloned.1.call-start = ((), (), s32[]{:S(2)}) async-start(), calls=%async_computation.20 | async-start | bytes 884736
  567.7 138.6 %reduce-scatter.54.cloned.1.call-start = ((), (), s32[]{:S(2)}) async-start(), calls=%async_computation.21 | async-start | bytes 589824
  648.1 7.2 collective-permute-start.5
  666.3 82.9 %reduce-scatter.56.cloned.1.call-start = ((), (), s32[]{:S(2)}) async-start(), calls=%async_computation.22 | async-start | bytes 884736
  670.9 259.4 %all-reduce.5.cloned.1.call-start = ((), (), s32[]{:S(2)}) async-start(), calls=%async_computation.12 | async-start | bytes 786432 | tf_op jit(solution)/shard_map/psum | solution.py:20
  677.7 28.7 %copy-start.76 = (bf16[4,64,128]{2,1,0:T(8,128)(2,1)}, bf16[4,64,128]{2,1,0:T(8,128)(2,1)S(1)}, u32[]{:S(2)}) copy-start(bf16[4,64,128]{2,1,0:T(8,128)(2,1)S(1)} %convolution_convert_fusion.16) | copy-start | bytes 196612
  677.7 28.7 %copy-start.16 = (bf16[1,1536,256]{2,1,0:T(8,128)(2,1)S(1)}, bf16[1,1536,256]{2,1,0:T(8,128)(2,1)}, u32[]{:S(2)}) copy-start(bf16[1,1536,256]{2,1,0:T(8,128)(2,1)} %param.11) | copy-start | bytes 2359300
  708.8 42.2 %copy-start.48 = (bf16[128,1536]{1,0:T(8,128)(2,1)S(1)}, bf16[128,1536]{1,0:T(8,128)(2,1)}, u32[]{:S(2)}) copy-start(bf16[128,1536]{1,0:T(8,128)(2,1)} %copy-done.47) | copy-start | bytes 1179652
  752.1 368.2 %reduce-scatter.38.cloned.1.call-start = ((), (), s32[]{:S(2)}) async-start(), calls=%async_computation.13 | async-start | bytes 1597440 | tf_op jit(solution)/shard_map/reduce_scatter | solution.py:219
  756.5 682.6 %reduce-scatter.40.cloned.1.call-start = ((), (), s32[]{:S(2)}) async-start(), calls=%async_computation.14 | async-start | bytes 1597440 | tf_op jit(solution)/shard_map/reduce_scatter | solution.py:220
  759.8 1000.1 %reduce-scatter.60.cloned.1.call-start = ((), (), s32[]{:S(2)}) async-start(), calls=%async_computation.24 | async-start | bytes 2396160
  764.8 1316.3 %reduce-scatter.58.cloned.1.call-start = ((), (), s32[]{:S(2)}) async-start(), calls=%async_computation.23 | async-start | bytes 2396160
  (84 other events, 163.8 us)
Sparse Core Ops, SparseCore 0:
  350.0 44.2 reduce-scatter.41
  396.9 40.1 reduce-scatter.43
  458.9 40.0 reduce-scatter.45
  501.4 40.1 reduce-scatter.47
  562.7 39.9 reduce-scatter.49
  605.2 40.2 reduce-scatter.51
  666.4 39.9 reduce-scatter.53
  708.9 40.2 reduce-scatter.55
  752.2 43.3 all-reduce.4
  798.5 321.7 reduce-scatter.37
  1123.4 315.6 reduce-scatter.39
  1442.1 317.7 reduce-scatter.59
  1763.0 318.0 reduce-scatter.57
where the time goes:
time: 2100 us; the launch traced here: 2090 us
  waiting for transfers between devices  1470 us (70%)
  blocking collectives  399 us (19%)
  matrix products  101 us (5%)
  local copies, waits for them, and re-layouts  69.9 us (3%)
    unnamed x23, waiting for transfers between devices  929 us
    reduce_scatter x1, waiting for transfers between devices, shards(): lax.psum_scatter(grad_key_w[None], ('dp', 'seq'), scatter_dimension=1, ti...  319 us
    reduce_scatter x1, waiting for transfers between devices, shards(): lax.psum_scatter(grad_query_w[None], ('dp', 'seq'), scatter_dimension=1,...  188 us
    unnamed x1, blocking collectives  158 us
    all_gather x4, blocking collectives, forward_layer(): lax.all_gather(value_local, 'seq', axis=0, tiled=True)  121 us
    all_gather x4, blocking collectives, forward_layer(): lax.all_gather(key_local, 'seq', axis=0, tiled=True)  120 us
  transfers between devices with their start and end apart: 19, of which 18 were waited for; matrix products, arithmetic and copies ran while one was open for 3% of the time, Pallas kernels for 0%

commit v1 on v0

--- a/solution.py
+++ b/solution.py
@@ -66,7 +66,9 @@
     )
     key_all, value_all = (
         lax.all_gather(key_local, "seq", axis=0, tiled=True),
-        lax.all_gather(value_local, "seq", axis=0, tiled=True),
+        jnp.concatenate(
+            lax.all_to_all(jnp.stack([value_local] * lax.axis_size("seq")), "seq", 0, 0), axis=0
+        ),
     )
     expo = exp_scores_of(query_local, key_all)
     totals = jnp.sum(expo, axis=-1)

time: 2100 us -> 2030 us (0.967)
  blocking collectives: 399 us -> 291 us
    all_gather x4 -> x0, blocking collectives: 121 us -> none  [forward_layer(): lax.all_gather(value_local, 'seq', axis=0, tiled=True)]
  transfers between devices with their start and end apart: 19 -> 23, of which waited for: 18 -> 18; matrix products, arithmetic and copies ran while one was open for 3% -> 5% of each run, Pallas kernels for 0% -> 0%
where the time goes in v1:
time: 2030 us; the launch traced here: 2020 us
  waiting for transfers between devices  1470 us (72%)
  blocking collectives  291 us (14%)
  matrix products  115 us (6%)
  local copies, waits for them, and re-layouts  82.3 us (4%)
  starting transfers between devices  30.2 us (1%)
    unnamed x23, waiting for transfers between devices  928 us
    reduce_scatter x1, waiting for transfers between devices, shards(): lax.psum_scatter(grad_key_w[None], ('dp', 'seq'), scatter_dimension=1, ti...  318 us
    reduce_scatter x1, waiting for transfers between devices, shards(): lax.psum_scatter(grad_query_w[None], ('dp', 'seq'), scatter_dimension=1,...  188 us
    unnamed x1, blocking collectives  158 us
    all_gather x4, blocking collectives, forward_layer(): lax.all_gather(key_local, 'seq', axis=0, tiled=True)  132 us
  transfers between devices with their start and end apart: 23, of which 18 were waited for; matrix products, arithmetic and copies ran while one was open for 5% of the time, Pallas kernels for 0%

profile of v1, /device:TPU:16, one launch (start us, length us, event | category | flops | bytes accessed | tf_op | source)
XLA Modules:
  0.0 2023.6 jit_solution(524153620109669000)
XLA Ops:
  13.1 5.0 all-to-all-start
  19.6 34.4 %all_gather.12 = bf16[1024,256]{1,0:T(8,128)(2,1)S(1)} all-gather(bf16[128,256]{1,0:T(8,128)(2,1)S(1)} %convolution_convert_fusion.14), channel_id=1, replica_groups=mesh['dp'=8,'section'=4,'seq'=8] {'seq'}, dimensions={0}, use_global_device_ids=true | all-gather | bytes 589824 | tf_op jit(solution)/shard_map/all_gather | solution.py:68
  56.1 2.5 copy.60
  65.7 8.7 collective-permute-done
  83.2 4.2 all-to-all-start.1
  88.9 33.6 %all_gather.13 = bf16[1024,256]{1,0:T(8,128)(2,1)} all-gather(bf16[128,256]{1,0:T(8,128)(2,1)S(1)} %convolution_convert_fusion.12), channel_id=1, replica_groups=mesh['dp'=8,'section'=4,'seq'=8] {'seq'}, dimensions={0}, use_global_device_ids=true | all-gather | bytes 589824 | tf_op jit(solution)/shard_map/all_gather | solution.py:68
  124.6 2.9 fusion.15
  127.5 2.5 copy.64
  137.1 8.7 collective-permute-done.1
  154.7 4.2 all-to-all-start.2
  160.4 33.7 %all_gather.14 = bf16[1024,256]{1,0:T(8,128)(2,1)} all-gather(bf16[128,256]{1,0:T(8,128)(2,1)S(1)} %convolution_convert_fusion.10), channel_id=1, replica_groups=mesh['dp'=8,'section'=4,'seq'=8] {'seq'}, dimensions={0}, use_global_device_ids=true | all-gather | bytes 589824 | tf_op jit(solution)/shard_map/all_gather | solution.py:68
  196.1 2.9 fusion.17
  199.0 2.5 copy.68
  213.1 5.1 collective-permute-done.2
  226.0 30.7 %all_gather.15 = bf16[1024,256]{1,0:T(8,128)(2,1)S(1)} all-gather(bf16[128,256]{1,0:T(8,128)(2,1)S(1)} %convolution_convert_fusion.9), channel_id=1, replica_groups=mesh['dp'=8,'section'=4,'seq'=8] {'seq'}, dimensions={0}, use_global_device_ids=true | all-gather | bytes 589824 | tf_op jit(solution)/shard_map/all_gather | solution.py:68
  258.8 4.4 all-to-all-start.3
  263.2 3.5 fusion.20
  270.6 2.9 fusion.171
  273.5 2.9 copy.77
  294.6 35.3 %reduce-scatter.42.cloned.1.call-done = bf16[128,256]{1,0:T(8,128)(2,1)} async-done(((bf16[1024,256]{1,0:T(8,128)(2,1)}), bf16[128,256]{1,0:T(8,128)(2,1)}) %reduce-scatter.42.cloned.1.call-update) | async-done | bytes 65552
  329.9 2.4 convolution_add_fusion.7
  332.3 40.2 %reduce-scatter.44.cloned.1.call-done = bf16[128,384]{1,0:T(8,128)(2,1)} async-done(((bf16[1024,384]{1,0:T(8,128)(2,1)}), bf16[128,384]{1,0:T(8,128)(2,1)}) %reduce-scatter.44.cloned.1.call-update) | async-done | bytes 98320
  372.6 3.1 multiply_reduce_fusion
  378.0 5.1 collective-permute-done.3
  387.8 2.4 multiply_convert_fusion.2
  394.4 2.5 convolution_convert_fusion.2
  403.1 31.4 %reduce-scatter.46.cloned.1.call-done = bf16[128,256]{1,0:T(8,128)(2,1)} async-done(((bf16[1024,256]{1,0:T(8,128)(2,1)}), bf16[128,256]{1,0:T(8,128)(2,1)}) %reduce-scatter.46.cloned.1.call-update) | async-done | bytes 65552
  434.6 2.7 convolution_add_fusion.5
  437.2 39.9 %reduce-scatter.48.cloned.1.call-done = bf16[128,384]{1,0:T(8,128)(2,1)} async-done(((bf16[1024,384]{1,0:T(8,128)(2,1)}), bf16[128,384]{1,0:T(8,128)(2,1)}) %reduce-scatter.48.cloned.1.call-update) | async-done | bytes 98320
  477.2 2.4 multiply_reduce_fusion.1
  481.8 5.3 collective-permute-done.4
  491.7 2.4 multiply_convert_fusion.1
  498.3 2.5 convolution_convert_fusion.1
  507.1 31.4 %reduce-scatter.50.cloned.1.call-done = bf16[128,256]{1,0:T(8,128)(2,1)} async-done(((bf16[1024,256]{1,0:T(8,128)(2,1)}), bf16[128,256]{1,0:T(8,128)(2,1)}) %reduce-scatter.50.cloned.1.call-update) | async-done | bytes 65552
  538.5 2.7 convolution_add_fusion.3
  541.2 39.9 %reduce-scatter.52.cloned.1.call-done = bf16[128,384]{1,0:T(8,128)(2,1)} async-done(((bf16[1024,384]{1,0:T(8,128)(2,1)}), bf16[128,384]{1,0:T(8,128)(2,1)}) %reduce-scatter.52.cloned.1.call-update) | async-done | bytes 98320
  581.1 2.5 multiply_reduce_fusion.2
  585.7 5.3 collective-permute-done.5
  609.0 2.5 fusion.174
  614.9 27.2 %reduce-scatter.54.cloned.1.call-done = bf16[128,256]{1,0:T(8,128)(2,1)} async-done(((bf16[1024,256]{1,0:T(8,128)(2,1)}), bf16[128,256]{1,0:T(8,128)(2,1)}) %reduce-scatter.54.cloned.1.call-update) | async-done | bytes 65552
  642.1 2.4 convolution_add_fusion.1
  644.6 40.2 %reduce-scatter.56.cloned.1.call-done = bf16[128,384]{1,0:T(8,128)(2,1)} async-done(((bf16[1024,384]{1,0:T(8,128)(2,1)}), bf16[128,384]{1,0:T(8,128)(2,1)}) %reduce-scatter.56.cloned.1.call-update) | async-done | bytes 98320
  689.1 3.1 fusion.8
  707.5 158.1 %all-reduce = f32[1,1536]{1,0:T(1,128)S(1)} all-reduce(f32[1,1536]{1,0:T(1,128)S(1)} %select_n.365), channel_id=10, replica_groups=mesh['dp'=8,'section'=4,'seq'=8] {'dp','seq'}, use_global_device_ids=true, to_apply=%region_37.38.clone | all-reduce | flops 1536 | bytes 12288
  867.8 188.3 %reduce-scatter.38.cloned.1.call-done = f32[1,24,256]{2,1,0:T(8,128)} async-done(((f32[1,1536,256]{2,1,0:T(8,128)}), f32[1,24,256]{2,1,0:T(8,128)}) %reduce-scatter.38.cloned.1.call-update) | async-done | bytes 24592 | tf_op jit(solution)/shard_map/reduce_scatter | solution.py:221
  1056.0 318.5 %reduce-scatter.40.cloned.1.call-done = f32[1,24,256]{2,1,0:T(8,128)} async-done(((f32[1,1536,256]{2,1,0:T(8,128)}), f32[1,24,256]{2,1,0:T(8,128)}) %reduce-scatter.40.cloned.1.call-update) | async-done | bytes 24592 | tf_op jit(solution)/shard_map/reduce_scatter | solution.py:222
  1374.5 321.0 %reduce-scatter.60.cloned.1.call-done = f32[1,24,384]{2,1,0:T(8,128)} async-done(((f32[1,1536,384]{2,1,0:T(8,128)}), f32[1,24,384]{2,1,0:T(8,128)}) %reduce-scatter.60.cloned.1.call-update) | async-done | bytes 36880
  1695.5 321.4 %reduce-scatter.58.cloned.1.call-done = f32[1,24,384]{2,1,0:T(8,128)} async-done(((f32[1,1536,384]{2,1,0:T(8,128)}), f32[1,24,384]{2,1,0:T(8,128)}) %reduce-scatter.58.cloned.1.call-update) | async-done | bytes 36880
  (387 shorter events, 169.9 us)
Async XLA Ops:
  8.4 10.8 copy-start.95
  9.7 9.5 copy-start.104
  10.4 7.7 copy-start.8
  10.4 7.7 copy-start.21
  12.1 7.1 copy-start.13
  13.1 42.9 %all-to-all-start = ((bf16[8,128,384]{1,2,0:T(8,128)(2,1)}), bf16[8,128,384]{1,2,0:T(8,128)(2,1)}, u32[]{:S(2)}, u32[]{:S(2)}) async-start(bf16[8,128,384]{1,2,0:T(8,128)(2,1)} %stack.8), calls=%async_computation | async-start | bytes 1572864 | tf_op jit(solution)/shard_map/all_to_all | solution.py:70
  63.2 11.2 copy-start.51
  63.7 10.6 collective-permute-start
  74.3 60.3 %copy-start.23 = (bf16[128,1536]{1,0:T(8,128)(2,1)}, bf16[128,1536]{1,0:T(8,128)(2,1)S(1)}, u32[]{:S(2)}) copy-start(bf16[128,1536]{1,0:T(8,128)(2,1)S(1)} %collective-permute-done) | copy-start | bytes 1179652
  74.7 8.5 copy-start.93
  83.2 44.3 %all-to-all-start.1 = ((bf16[8,128,384]{1,2,0:T(8,128)(2,1)}), bf16[8,128,384]{1,2,0:T(8,128)(2,1)}, u32[]{:S(2)}, u32[]{:S(2)}) async-start(bf16[8,128,384]{1,2,0:T(8,128)(2,1)} %stack.9), calls=%async_computation.1 | async-start | bytes 1572864 | tf_op jit(solution)/shard_map/all_to_all | solution.py:70
  127.5 7.0 copy-start.85
  134.6 11.2 copy-start.54
  135.1 10.6 collective-permute-start.1
  145.7 60.3 %copy-start.25 = (bf16[128,1536]{1,0:T(8,128)(2,1)}, bf16[128,1536]{1,0:T(8,128)(2,1)S(1)}, u32[]{:S(2)}) copy-start(bf16[128,1536]{1,0:T(8,128)(2,1)S(1)} %collective-permute-done.1) | copy-start | bytes 1179652
  146.1 8.5 copy-start.94
  154.7 44.3 %all-to-all-start.2 = ((bf16[8,128,384]{1,2,0:T(8,128)(2,1)}), bf16[8,128,384]{1,2,0:T(8,128)(2,1)}, u32[]{:S(2)}, u32[]{:S(2)}) async-start(bf16[8,128,384]{1,2,0:T(8,128)(2,1)} %stack.10), calls=%async_computation.2 | async-start | bytes 1572864 | tf_op jit(solution)/shard_map/all_to_all | solution.py:70
  199.0 7.0 copy-start.86
  206.1 12.5 copy-start.92
  207.4 10.8 collective-permute-start.2
  226.0 37.2 %copy-start.77 = (bf16[128,256]{0,1:T(8,128)(2,1)S(1)}, bf16[128,256]{0,1:T(8,128)(2,1)}, u32[]{:S(2)}) copy-start(bf16[128,256]{0,1:T(8,128)(2,1)} %copy.74) | copy-start | bytes 196612
  258.8 8.0 copy-start.28
  258.8 8.0 copy-start.29
  258.8 14.7 all-to-all-start.3
  263.1 66.7 %reduce-scatter.42.cloned.1.call-start = ((), (), s32[]{:S(2)}) async-start(), calls=%async_computation.19 | async-start | bytes 589824
  267.8 15.1 copy-start.45
  273.5 12.8 copy-start.3
  286.2 86.4 %reduce-scatter.44.cloned.1.call-start = ((), (), s32[]{:S(2)}) async-start(), calls=%async_computation.20 | async-start | bytes 884736
  290.8 143.8 %reduce-scatter.46.cloned.1.call-start = ((), (), s32[]{:S(2)}) async-start(), calls=%async_computation.21 | async-start | bytes 589824
  292.6 37.2 %copy-start.14 = (bf16[1,1536,256]{2,1,0:T(8,128)(2,1)S(1)}, bf16[1,1536,256]{2,1,0:T(8,128)(2,1)}, u32[]{:S(2)}) copy-start(bf16[1,1536,256]{2,1,0:T(8,128)(2,1)} %param.11) | copy-start | bytes 2359300
  292.7 79.9 %copy-start.22 = (bf16[1,128,1536]{2,1,0:T(8,128)(2,1)S(1)}, bf16[1,128,1536]{2,1,0:T(8,128)(2,1)}, u32[]{:S(2)}) copy-start(bf16[1,128,1536]{2,1,0:T(8,128)(2,1)} %param.7) | copy-start | bytes 1179652
  332.3 43.3 %copy-start.87 = (f32[128]{0:T(128)S(1)}, f32[128]{0:T(128)}, u32[]{:S(2)}) copy-start(f32[128]{0:T(128)} %get-tuple-element.28) | copy-start | bytes 1540
  375.9 7.2 collective-permute-start.3
  394.3 82.8 %reduce-scatter.48.cloned.1.call-start = ((), (), s32[]{:S(2)}) async-start(), calls=%async_computation.22 | async-start | bytes 884736
  399.2 139.3 %reduce-scatter.50.cloned.1.call-start = ((), (), s32[]{:S(2)}) async-start(), calls=%async_computation.23 | async-start | bytes 589824
  479.9 7.2 collective-permute-start.4
  498.3 82.8 %reduce-scatter.52.cloned.1.call-start = ((), (), s32[]{:S(2)}) async-start(), calls=%async_computation.24 | async-start | bytes 884736
  503.2 139.0 %reduce-scatter.54.cloned.1.call-start = ((), (), s32[]{:S(2)}) async-start(), calls=%async_computation.25 | async-start | bytes 589824
  583.8 7.2 collective-permute-start.5
  602.0 82.9 %reduce-scatter.56.cloned.1.call-start = ((), (), s32[]{:S(2)}) async-start(), calls=%async_computation.26 | async-start | bytes 884736
  606.6 259.6 %all-reduce.5.cloned.1.call-start = ((), (), s32[]{:S(2)}) async-start(), calls=%async_computation.16 | async-start | bytes 786432 | tf_op jit(solution)/shard_map/psum | solution.py:20
  613.6 28.5 %copy-start.68 = (bf16[4,64,128]{2,1,0:T(8,128)(2,1)}, bf16[4,64,128]{2,1,0:T(8,128)(2,1)S(1)}, u32[]{:S(2)}) copy-start(bf16[4,64,128]{2,1,0:T(8,128)(2,1)S(1)} %convolution_convert_fusion.16) | copy-start | bytes 196612
  613.6 28.5 %copy-start.15 = (bf16[1,1536,256]{2,1,0:T(8,128)(2,1)S(1)}, bf16[1,1536,256]{2,1,0:T(8,128)(2,1)}, u32[]{:S(2)}) copy-start(bf16[1,1536,256]{2,1,0:T(8,128)(2,1)} %param.11) | copy-start | bytes 2359300
  644.6 42.1 %copy-start.43 = (bf16[128,1536]{1,0:T(8,128)(2,1)S(1)}, bf16[128,1536]{1,0:T(8,128)(2,1)}, u32[]{:S(2)}) copy-start(bf16[128,1536]{1,0:T(8,128)(2,1)} %copy-done.42) | copy-start | bytes 1179652
  687.8 368.3 %reduce-scatter.38.cloned.1.call-start = ((), (), s32[]{:S(2)}) async-start(), calls=%async_computation.17 | async-start | bytes 1597440 | tf_op jit(solution)/shard_map/reduce_scatter | solution.py:221
  692.2 682.3 %reduce-scatter.40.cloned.1.call-start = ((), (), s32[]{:S(2)}) async-start(), calls=%async_computation.18 | async-start | bytes 1597440 | tf_op jit(solution)/shard_map/reduce_scatter | solution.py:222
  695.5 1000.0 %reduce-scatter.60.cloned.1.call-start = ((), (), s32[]{:S(2)}) async-start(), calls=%async_computation.28 | async-start | bytes 2396160
  700.4 1316.4 %reduce-scatter.58.cloned.1.call-start = ((), (), s32[]{:S(2)}) async-start(), calls=%async_computation.27 | async-start | bytes 2396160
  (83 other events, 179.3 us)
Sparse Core Ops, SparseCore 0:
  286.3 43.4 reduce-scatter.41
  332.4 40.1 reduce-scatter.43
  394.4 40.0 reduce-scatter.45
  437.0 40.1 reduce-scatter.47
  498.4 40.0 reduce-scatter.49
  540.9 40.1 reduce-scatter.51
  602.1 39.9 reduce-scatter.53
  644.7 40.1 reduce-scatter.55
  687.9 43.3 all-reduce.4
  734.2 321.7 reduce-scatter.37
  1059.1 315.3 reduce-scatter.39
  1377.4 318.0 reduce-scatter.59
  1698.6 318.2 reduce-scatter.57
